TPU v7x, 256 devices: a whole 4x4x8 slice. The times are simulated.
256 devices in a mesh: outer: 32 (over z, x), inner: 8 (over y, core).
Axes of the slice: x: 4, y: 4, z: 8, core: 2. Of those that a mesh axis runs over, the one named last changes fastest.
Arguments:
- queries: bfloat16 [32768, 2048], P(('outer', 'inner')), may hold values from -5 to 5
- key_rows: bfloat16 [32768, 2048], P(('outer', 'inner')), may hold values from -5 to 5
- value_rows: bfloat16 [32768, 2048], P(('outer', 'inner')), may hold values from -6 to 6
- out_grad: bfloat16 [32768, 2048], P(('outer', 'inner')), may hold values from -6 to 6
- log_gate: float32 [16, 32768], P(None, ('outer', 'inner')), may hold values from -1 to 0
Outputs:
- mixed_out: bfloat16 [32768, 2048], P(('outer', 'inner'))
- query_grad: bfloat16 [32768, 2048], P(('outer', 'inner'))
- key_grad: bfloat16 [32768, 2048], P(('outer', 'inner'))
- value_grad: bfloat16 [32768, 2048], P(('outer', 'inner'))
All inputs are finite; a program needn't handle non-finite values.
Results may differ from a plain program's by a relative error of at most 0.007.
Values may be sent and summed in bfloat16 or wider, within the bound.
No kernel may reach another device: no remote copies, remote signals or barrier semaphores. Data moves between devices by JAX's collectives and lax.ppermute only.
A program may use at most 256 MiB of HBM per device.

v0:
```python
import jax
import jax.numpy as jnp
from jax import lax
from jax.sharding import PartitionSpec as P

W = 64


def from_behind(value, axis, steps):
    count = lax.axis_size(axis)
    first, last = (max(0, -steps), min(count, count - steps))
    return lax.ppermute(value, axis, [(source, source + steps) for source in range(first, last)])


def carried_in(part, axis, combine, identity, reverse):
    count = lax.axis_size(axis)
    place = lax.axis_index(axis)
    ahead = count - 1 - place if reverse else place
    gathered = jax.tree.map(lambda a: lax.all_gather(a, axis), part)
    state = jax.tree.map(lambda a, e: jnp.zeros_like(a) + jnp.asarray(e, a.dtype), part, identity)

    def one(hop, state):
        source = count - 1 - hop if reverse else hop
        return combine(
            state, jax.tree.map(lambda a: lax.dynamic_index_in_dim(a, source, 0, False), gathered)
        )

    return lax.fori_loop(0, ahead, one, state)


def low_product(form, left, right):
    return jnp.einsum(form, left, right, preferred_element_type=jnp.float32)


def high_product(form, left, right):
    return jnp.einsum(form, left, right, precision=lax.Precision.HIGHEST)


def local_states(query_blk, key_blk, value_blk, grad_blk, gate_rows):
    cumul_gate = jnp.cumsum(gate_rows, axis=1)
    last_cumul = cumul_gate[:, -1:]
    block_decay = jnp.exp(cumul_gate[:, -1])
    tail_weight = jnp.exp(last_cumul - cumul_gate).T
    head_weight = jnp.exp(cumul_gate).T
    state_local = high_product(
        "thf,the->hfe",
        key_blk.astype(jnp.float32) * tail_weight[:, :, None],
        value_blk.astype(jnp.float32),
    )
    grad_local = high_product(
        "thf,the->hfe",
        query_blk.astype(jnp.float32) * head_weight[:, :, None],
        grad_blk.astype(jnp.float32),
    )
    return (block_decay, state_local, grad_local)


def block_terms(
    query_blk,
    key_blk,
    value_blk,
    grad_blk,
    gate_rows,
    state_in,
    grad_after,
    key_halo,
    value_halo,
    halo_live,
    lin_scale,
):
    row_count = query_blk.shape[0]
    halo_rows = key_halo.shape[0]
    head_size = query_blk.shape[2]
    cumul_gate = jnp.cumsum(gate_rows, axis=1)
    last_cumul = cumul_gate[:, -1:]
    head_weight = jnp.exp(cumul_gate).T
    tail_weight = jnp.exp(last_cumul - cumul_gate).T
    query_pos = jnp.arange(row_count)[:, None]
    key_pos = jnp.arange(row_count)[None, :]
    causal_mask = (key_pos <= query_pos)[None]
    gap_logs = cumul_gate[:, :, None] - cumul_gate[:, None, :]
    decay_grid = jnp.where(causal_mask, jnp.exp(jnp.where(causal_mask, gap_logs, 0.0)), 0.0)
    lin_weight = (low_product("thf,shf->hts", query_blk, key_blk) * decay_grid).astype(jnp.bfloat16)
    query_decayed = query_blk.astype(jnp.float32) * head_weight[:, :, None]
    lin_out = low_product("hts,she->the", lin_weight, value_blk) + high_product(
        "thf,hfe->the", query_decayed, state_in
    )
    ext_keys = jnp.concatenate([key_halo, key_blk], axis=0)
    ext_values = jnp.concatenate([value_halo, value_blk], axis=0)
    ext_pos = jnp.arange(row_count + halo_rows)[None, :]
    in_band = (
        (ext_pos > query_pos)
        & (ext_pos <= query_pos + halo_rows)
        & ((ext_pos >= halo_rows) | halo_live)
    )[None]
    logits = low_product("thf,jhf->htj", query_blk, ext_keys) * head_size ** (-0.5)
    masked_logits = jnp.where(in_band, logits, -jnp.inf)
    row_max = jnp.max(masked_logits, axis=2, keepdims=True)
    expo_terms = jnp.exp(masked_logits - row_max)
    win_prob = expo_terms / jnp.sum(expo_terms, axis=2, keepdims=True)
    prob_low = win_prob.astype(jnp.bfloat16)
    win_out = low_product("htj,jhe->the", prob_low, ext_values)
    output = (lin_scale * lin_out + win_out).astype(jnp.bfloat16)
    grad_weight = (low_product("the,she->hts", grad_blk, value_blk) * decay_grid).astype(
        jnp.bfloat16
    )
    grad_decayed = grad_blk.astype(jnp.float32) * head_weight[:, :, None]
    query_lin = low_product("hts,shf->thf", grad_weight, key_blk) + high_product(
        "the,hfe->thf", grad_decayed, state_in
    )
    value_tail = value_blk.astype(jnp.float32) * tail_weight[:, :, None]
    key_tail = key_blk.astype(jnp.float32) * tail_weight[:, :, None]
    key_lin = low_product("hts,thf->shf", grad_weight, query_blk) + high_product(
        "she,hfe->shf", value_tail, grad_after
    )
    value_lin = low_product("hts,the->she", lin_weight, grad_blk) + high_product(
        "shf,hfe->she", key_tail, grad_after
    )
    prob_grad = low_product("the,jhe->htj", grad_blk, ext_values)
    row_delta = jnp.sum(win_prob * prob_grad, axis=2, keepdims=True)
    logit_grad = (win_prob * (prob_grad - row_delta) * head_size ** (-0.5)).astype(jnp.bfloat16)
    query_win = low_product("htj,jhf->thf", logit_grad, ext_keys)
    key_ext = low_product("htj,thf->jhf", logit_grad, query_blk)
    value_ext = low_product("htj,the->jhe", prob_low, grad_blk)
    query_grad = (lin_scale * query_lin + query_win).astype(jnp.bfloat16)
    key_local = lin_scale * key_lin + key_ext[halo_rows:]
    value_local = lin_scale * value_lin + value_ext[halo_rows:]
    return (output, query_grad, key_local, value_local, key_ext[:halo_rows], value_ext[:halo_rows])


def forward_merge(earlier_part, later_part):
    return (
        earlier_part[0] * later_part[0],
        later_part[0][:, None, None] * earlier_part[1] + later_part[1],
    )


def backward_merge(earlier_part, later_part):
    return (
        earlier_part[0] * later_part[0],
        later_part[1] + later_part[0][:, None, None] * earlier_part[1],
    )


def run_forward(running, element):
    return (forward_merge(running, element), running)


def run_backward(running, element):
    return (backward_merge(running, element), running)


def select_mine(bundle, inner_pos):
    return tuple(
        (lax.dynamic_index_in_dim(member, inner_pos, 0, keepdims=False) for member in bundle)
    )


def per_device(queries, key_rows, value_rows, out_grad, log_gate):
    row_count = queries.shape[0]
    head_count = log_gate.shape[0]
    head_size = queries.shape[1] // head_count
    devices = lax.axis_size("outer") * lax.axis_size("inner")
    lin_scale = (head_size * row_count * devices) ** (-0.5)
    block_shape = (row_count, head_count, head_size)
    query_blk = queries.reshape(block_shape)
    key_blk = key_rows.reshape(block_shape)
    value_blk = value_rows.reshape(block_shape)
    grad_blk = out_grad.reshape(block_shape)
    block_decay, state_local, grad_local = local_states(
        query_blk, key_blk, value_blk, grad_blk, log_gate
    )
    key_halo, value_halo = from_behind((key_blk[-W:], value_blk[-W:]), ("outer", "inner"), 1)
    position = lax.axis_index("outer") * lax.axis_size("inner") + lax.axis_index("inner")
    identity_pair = (
        jnp.ones((head_count,), jnp.float32),
        jnp.zeros((head_count, head_size, head_size), jnp.float32),
    )
    gathered = (
        lax.all_gather(block_decay[None], "inner", axis=0, tiled=True),
        lax.all_gather(state_local[None], "inner", axis=0, tiled=True),
        lax.all_gather(grad_local[None], "inner", axis=0, tiled=True),
    )
    group_decay, group_state, group_grad = gathered
    total_forward, before_forward = lax.scan(run_forward, identity_pair, (group_decay, group_state))
    total_backward, after_backward = lax.scan(
        run_backward, identity_pair, (group_decay, group_grad), reverse=True
    )
    inner_pos = lax.axis_index("inner")
    mine_forward = select_mine(before_forward, inner_pos)
    mine_backward = select_mine(after_backward, inner_pos)
    outer_forward = carried_in(total_forward, "outer", forward_merge, identity_pair, False)
    outer_backward = carried_in(total_backward, "outer", backward_merge, identity_pair, True)
    forward_pair = forward_merge(outer_forward, mine_forward)
    backward_pair = backward_merge(outer_backward, mine_backward)
    output, query_grad, key_local, value_local, key_back, value_back = block_terms(
        query_blk,
        key_blk,
        value_blk,
        grad_blk,
        log_gate,
        forward_pair[1],
        backward_pair[1],
        key_halo,
        value_halo,
        position > 0,
        lin_scale,
    )
    key_return, value_return = (
        from_behind(key_back.astype(jnp.bfloat16), ("outer", "inner"), -1).astype(key_back.dtype),
        from_behind(value_back.astype(jnp.bfloat16), ("outer", "inner"), -1).astype(
            value_back.dtype
        ),
    )
    key_grad = key_local.at[-W:].add(key_return).astype(jnp.bfloat16)
    value_grad = value_local.at[-W:].add(value_return).astype(jnp.bfloat16)
    flat_shape = (row_count, head_count * head_size)
    return (
        output.reshape(flat_shape),
        query_grad.reshape(flat_shape),
        key_grad.reshape(flat_shape),
        value_grad.reshape(flat_shape),
    )


def solution(mesh):
    placed = (
        P(("outer", "inner"), None),
        P(("outer", "inner"), None),
        P(("outer", "inner"), None),
        P(("outer", "inner"), None),
        P(None, ("outer", "inner")),
    )
    return jax.shard_map(
        per_device,
        mesh=mesh,
        in_specs=placed,
        out_specs=(
            P(("outer", "inner"), None),
            P(("outer", "inner"), None),
            P(("outer", "inner"), None),
            P(("outer", "inner"), None),
        ),
        check_vma=False,
    )
```

profile of v0, /device:TPU:230, one launch (start us, length us, event | category | flops | bytes accessed | tf_op | source)
XLA Modules:
  0.0 660.7 jit_solution(8102679605573216670)
XLA Ops:
  18.4 15.5 %all-reduce = f32[128]{0:T(128)S(1)} all-reduce(f32[128]{0:T(128)S(1)} %dynamic-update-slice.6), channel_id=2, replica_groups=mesh['outer'=32,'inner'=8] {'inner'}, use_global_device_ids=true, to_apply=%add | all-reduce | flops 128 | bytes 1024
  34.0 32.2 %all-gather.16.cloned.1.call-done = f32[128,128,128]{2,1,0:T(8,128)} async-done(((f32[16,128,128]{2,1,0:T(8,128)}), f32[128,128,128]{2,1,0:T(8,128)}) %all-gather.16.cloned.1.call-update) | async-done | bytes 8388624 | tf_op jit(solution)/shard_map/all_gather | solution.py:182
  66.1 4.4 broadcast.104.clone.1
  70.5 21.0 %while.69 = (s32[]{:T(128)}, f32[16]{0:T(128)S(1)}, f32[16,128,128]{2,1,0:T(8,128)S(1)}, f32[8,16]{1,0:T(8,128)S(1)}, f32[8,16,128,128]{3,2,1,0:T(8,128)}, /*ind...) while((s32[]{:T(128)}, f32[16]{0:T(128)S(1)}, ...), condition=%wide.region_9.10_spmd.clone, body=%wide.region_8.9_spmd.clone.sunk | while | flops 1048612 | bytes 5243533 | solution.py:186
  92.6 27.8 %all-gather.12.cloned.1.call-done = f32[128,128,128]{2,1,0:T(8,128)} async-done(((f32[16,128,128]{2,1,0:T(8,128)}), f32[128,128,128]{2,1,0:T(8,128)}) %all-gather.12.cloned.1.call-update) | async-done | bytes 8388624 | tf_op jit(solution)/shard_map/all_gather | solution.py:181
  120.4 4.3 broadcast.104.clone
  124.7 20.6 %while.68 = (s32[]{:T(128)}, f32[16]{0:T(128)S(1)}, f32[16,128,128]{2,1,0:T(8,128)S(1)}, f32[8,16]{1,0:T(8,128)S(1)}, f32[8,16,128,128]{3,2,1,0:T(8,128)}, /*ind...) while((s32[]{:T(128)}, f32[16]{0:T(128)S(1)}, ...), condition=%wide.region_2.3_spmd.clone, body=%wide.region_1.2_spmd.clone.sunk | while | flops 1048611 | bytes 5244021 | solution.py:185
  151.2 2.5 collective-permute-start
  160.0 2.6 collective-permute-done.1
  162.6 2.7 fusion.70
  165.3 3.3 convolution_bitcast_fusion
  170.8 2.5 collective-permute-start.3
  175.8 4.8 convolution_bitcast_fusion.1
  185.4 72.2 %all-reduce.3 = (f32[512]{0:T(512)S(1)}, f32[512]{0:T(512)S(1)}) all-reduce(f32[512]{0:T(512)S(1)} %dynamic-update-slice.7, f32[512]{0:T(512)S(1)} %dynamic-update-slice.8), channel_id=4, replica_groups=mesh['outer'=32,'inner'=8] {'outer'}, use_global_device_ids=true, to_apply=%add.1 | all-reduce | flops 1024 | bytes 8192
  257.7 100.4 %all-gather.18.cloned.1.call-done = f32[512,128,128]{2,1,0:T(8,128)} async-done(((f32[16,128,128]{2,1,0:T(8,128)}), f32[512,128,128]{2,1,0:T(8,128)}) %all-gather.18.cloned.1.call-update) | async-done | bytes 33554448 | tf_op jit(solution)/shard_map/all_gather | solution.py:19
  358.5 3.3 convolution_bitcast_fusion.4
  365.6 7.0 %scatter-add.9 = f32[128,16,128]{0,2,1:T(8,128)} dynamic-update-slice(f32[128,16,128]{0,2,1:T(8,128)} %copy-done.2, f32[64,16,128]{0,2,1:T(8,128)} %slice_add_fusion, s32[]{:T(128)} %constant.187.clone.1, s32[]{:T(128)} %constant.180.clone.1, s32[]{:T(128)} %constant.180.clone.1) | dynamic-update-slice | bytes 1048580 | tf_op jit(solution)/shard_map/scatter-add | solution.py:216
  375.1 2.8 convolution_bitcast_fusion.5
  379.7 5.1 scatter-add.6
  385.9 204.5 %all-gather.14.cloned.1.call-done = f32[512,128,128]{2,1,0:T(8,128)} async-done(((f32[16,128,128]{2,1,0:T(8,128)}), f32[512,128,128]{2,1,0:T(8,128)}) %all-gather.14.cloned.1.call-update) | async-done | bytes 33554448 | tf_op jit(solution)/shard_map/all_gather | solution.py:19
  590.6 46.6 %while.66 = (s32[]{:T(128)}, f32[16,128,128]{2,1,0:T(8,128)S(1)}, s32[]{:T(128)}, f32[32,16]{1,0:T(8,128)S(1)}, f32[32,16,128,128]{3,2,1,0:T(8,128)}, /*index=5*/s32[]{:T(128)}, s32[]{:T(128)}, s32[]{:T(128)}) while((s32[]{:T(128)}, f32[16,128,128]{2,1,0:T(8,128)S(1)}, s32[]{:T(128)}, f32[32,16]{1,0:T(8,128)S(1)}, ...), condition=%wide.region_4.5_spmd, body=%wide.region_3.4_spmd.sunk | while | flops 524293 | bytes 3146047 | solution.py:28
  637.1 3.6 fusion.20
  640.7 4.3 fusion.26
  646.5 4.2 fusion.22
  (232 shorter events, 133.4 us)
Async XLA Ops:
  7.2 59.0 %all-gather.16.cloned.1.call-start = ((), (), s32[]{:S(2)}) async-start(), calls=%async_computation.2 | async-start | bytes 9437184 | tf_op jit(solution)/shard_map/all_gather | solution.py:182
  11.1 2.3 copy-start.11
  13.3 1.0 copy-start.12
  13.3 107.1 %all-gather.12.cloned.1.call-start = ((), (), s32[]{:S(2)}) async-start(), calls=%async_computation | async-start | bytes 9437184 | tf_op jit(solution)/shard_map/all_gather | solution.py:181
  14.6 2.3 copy-start.17
  16.8 341.3 %all-gather.18.cloned.1.call-start = ((), (), s32[]{:S(2)}) async-start(), calls=%async_computation.3 | async-start | bytes 34603008 | tf_op jit(solution)/shard_map/all_gather | solution.py:19
  92.5 498.0 %all-gather.14.cloned.1.call-start = ((), (), s32[]{:S(2)}) async-start(), calls=%async_computation.1 | async-start | bytes 34603008 | tf_op jit(solution)/shard_map/all_gather | solution.py:19
  146.3 8.1 %copy-start.16 = (u32[256]{0:T(256)S(1)}, u32[256]{0:T(256)}, u32[]{:S(2)}) copy-start(u32[256]{0:T(256)} %constant.203) | copy-start | bytes 3076
  148.0 14.6 %collective-permute-start.1 = (bf16[64,16,128]{2,0,1:T(8,128)(2,1)}, bf16[64,16,128]{2,0,1:T(8,128)(2,1)}, u32[]{:S(2)}, u32[]{:S(2)}) collective-permute-start(bf16[64,16,128]{2,0,1:T(8,128)(2,1)} %copy_bitcast_fusion), channel_id=1, source_target_pairs={{0,1},{1,2},{2,3},{3,4},{4,5},{5,6},{6,7},{7,8},{8,9},{9,10},{10,1... | collective-permute-start | bytes 786440 | tf_op jit(solution)/shard_map/ppermute | solution.py:12
  151.2 22.1 %collective-permute-start = (bf16[64,16,128]{2,0,1:T(8,128)(2,1)S(1)}, bf16[64,16,128]{2,0,1:T(8,128)(2,1)}, u32[]{:S(2)}, u32[]{:S(2)}) collective-permute-start(bf16[64,16,128]{2,0,1:T(8,128)(2,1)S(1)} %copy_bitcast_fusion.1), channel_id=1, source_target_pairs={{0,1},{1,2},{2,3},{3,4},{4,5},{5,6},{6,7},{7,8},{8,9},{9,10},{10,1... | collective-permute-start | bytes 786440 | tf_op jit(solution)/shard_map/ppermute | solution.py:12
  154.0 11.2 %copy-start.15 = (bf16[128,16,128]{2,0,1:T(8,128)(2,1)}, bf16[128,16,128]{2,0,1:T(8,128)(2,1)S(1)}, u32[]{:S(2)}) copy-start(bf16[128,16,128]{2,0,1:T(8,128)(2,1)S(1)} %copy.84) | copy-start | bytes 1572868
  154.3 19.0 %copy-start.5 = (bf16[128,16,128]{2,0,1:T(8,128)(2,1)}, bf16[128,16,128]{2,0,1:T(8,128)(2,1)S(1)}, u32[]{:S(2)}) copy-start(bf16[128,16,128]{2,0,1:T(8,128)(2,1)S(1)} %copy.82) | copy-start | bytes 1572868
  156.4 2.1 copy-start.9
  157.0 3.0 copy-start.7
  170.8 191.5 %collective-permute-start.3 = (bf16[64,16,128]{0,2,1:T(8,128)(2,1)}, bf16[64,16,128]{0,2,1:T(8,128)(2,1)}, u32[]{:S(2)}, u32[]{:S(2)}) collective-permute-start(bf16[64,16,128]{0,2,1:T(8,128)(2,1)} %slice.107), channel_id=1, source_target_pairs={{1,0},{2,1},{3,2},{4,3},{5,4},{6,5},{7,6},{8,7},{9,8},{10,9},{11,1... | collective-permute-start | bytes 786440 | tf_op jit(solution)/shard_map/ppermute | solution.py:12
  182.8 195.6 %collective-permute-start.2 = (bf16[64,16,128]{0,2,1:T(8,128)(2,1)}, bf16[64,16,128]{0,2,1:T(8,128)(2,1)}, u32[]{:S(2)}, u32[]{:S(2)}) collective-permute-start(bf16[64,16,128]{0,2,1:T(8,128)(2,1)} %slice.108), channel_id=1, source_target_pairs={{1,0},{2,1},{3,2},{4,3},{5,4},{6,5},{7,6},{8,7},{9,8},{10,9},{11,1... | collective-permute-start | bytes 786440 | tf_op jit(solution)/shard_map/ppermute | solution.py:12
  358.5 3.4 copy-start.10
  358.5 3.4 copy-start.14
  362.3 1.0 copy-start.2
  375.1 2.8 copy-start.8
  375.1 2.8 copy-start.13
  590.6 46.6 %copy-start.4 = (f32[128,16,128]{0,2,1:T(8,128)S(1)}, f32[128,16,128]{0,2,1:T(8,128)}, u32[]{:S(2)}) copy-start(f32[128,16,128]{0,2,1:T(8,128)} %convolution_bitcast_fusion.7) | copy-start | bytes 3145732
  645.0 1.4 copy-start.3
  646.5 4.2 copy-start.6
  (2 other events, 1.9 us)
Sparse Core Ops, SparseCore 0:
  13.5 52.6 all-gather.15
  68.0 52.3 all-gather.11
  123.0 235.1 all-gather.17
  360.6 229.8 all-gather.13
where the time goes:
time: 664 us; the launch traced here: 661 us
  waiting for transfers between devices  368 us (55%)
  other arithmetic  92.1 us (14%)
  blocking collectives  87.6 us (13%)
  matrix products  43.3 us (7%)
  local copies, waits for them, and re-layouts  43.1 us (6%)
  between operations  15.6 us (2%)
  starting transfers between devices  9.56 us (1%)
    all_gather x2, waiting for transfers between devices, carried_in(): gathered = jax.tree.map(lambda a: lax.all_gather(a, axis), part)  305 us
    unnamed x2, blocking collectives  87.6 us
    add x39, other arithmetic, forward_merge(): later_part[0][:, None, None] * earlier_part[1] + later_part[1]  56.4 us
    all_gather x1, waiting for transfers between devices, per_device(): lax.all_gather(grad_local[None], 'inner', axis=0, tiled=True)  32.2 us
    all_gather x1, waiting for transfers between devices, per_device(): lax.all_gather(state_local[None], 'inner', axis=0, tiled=True)  27.8 us
    dot_general x11, matrix products, low_product(): return jnp.einsum(form, left, right, preferred_element_type=jnp.float32)  22.3 us
    dot_general x6, matrix products, high_product(): return jnp.einsum(form, left, right, precision=lax.Precision.HIGHEST)  18.3 us
    dynamic_update_slice x16, other arithmetic, per_device(): lax.scan(run_forward, identity_pair, (group_decay, group_state))  17.3 us
  transfers between devices with their start and end apart: 8, of which 5 were waited for; matrix products, arithmetic and copies ran while one was open for 16% of the time, Pallas kernels for 0%

commit v1 on v0

--- a/solution.py
+++ b/solution.py
@@ -179,7 +179,10 @@
     gathered = (
         lax.all_gather(block_decay[None], "inner", axis=0, tiled=True),
         lax.all_gather(state_local[None], "inner", axis=0, tiled=True),
-        lax.all_gather(grad_local[None], "inner", axis=0, tiled=True),
+        jnp.concatenate(
+            lax.all_to_all(jnp.stack([grad_local[None]] * lax.axis_size("inner")), "inner", 0, 0),
+            axis=0,
+        ),
     )
     group_decay, group_state, group_grad = gathered
     total_forward, before_forward = lax.scan(run_forward, identity_pair, (group_decay, group_state))

time: 664 us -> 728 us (1.096)
  blocking collectives: 87.6 us -> 207 us
  waiting for transfers between devices: 368 us -> 300 us
  starting transfers between devices: 9.56 us -> 17.3 us
    unnamed x2, blocking collectives: 87.6 us -> 207 us
    all_gather x1 -> x0, waiting for transfers between devices: 32.2 us -> none  [per_device(): lax.all_gather(grad_local[None], 'inner', axis=0, tiled=True)]
    all_gather x1, waiting for transfers between devices: 27.8 us -> 0.02 us  [per_device(): lax.all_gather(state_local[None], 'inner', axis=0, tiled=True)]
  transfers between devices with their start and end apart: 8 -> 8, of which waited for: 5 -> 2; matrix products, arithmetic and copies ran while one was open for 16% -> 15% of each run, Pallas kernels for 0% -> 0%
where the time goes in v1:
time: 728 us; the launch traced here: 724 us
  waiting for transfers between devices  300 us (41%)
  blocking collectives  207 us (28%)
  other arithmetic  92.1 us (13%)
  local copies, waits for them, and re-layouts  48.3 us (7%)
  matrix products  42.5 us (6%)
  starting transfers between devices  17.3 us (2%)
  between operations  15.6 us (2%)
    all_gather x2, waiting for transfers between devices, carried_in(): gathered = jax.tree.map(lambda a: lax.all_gather(a, axis), part)  300 us
    unnamed x2, blocking collectives  207 us
    add x39, other arithmetic, forward_merge(): later_part[0][:, None, None] * earlier_part[1] + later_part[1]  56.6 us
    dot_general x11, matrix products, low_product(): return jnp.einsum(form, left, right, preferred_element_type=jnp.float32)  22.4 us
    dynamic_update_slice x16, other arithmetic, per_device(): lax.scan(run_forward, identity_pair, (group_decay, group_state))  17.3 us
    dot_general x6, matrix products, high_product(): return jnp.einsum(form, left, right, precision=lax.Precision.HIGHEST)  17.3 us
  transfers between devices with their start and end apart: 8, of which 2 were waited for; matrix products, arithmetic and copies ran while one was open for 15% of the time, Pallas kernels for 0%

profile of v1, /device:TPU:230, one launch (start us, length us, event | category | flops | bytes accessed | tf_op | source)
XLA Modules:
  0.0 724.5 jit_solution(6350064936128534855)
XLA Ops:
  15.9 4.3 stack.3
  20.2 5.2 all-to-all-start
  27.0 131.6 %all-reduce = f32[128]{0:T(128)S(1)} all-reduce(f32[128]{0:T(128)S(1)} %dynamic-update-slice.6), channel_id=2, replica_groups=mesh['outer'=32,'inner'=8] {'inner'}, use_global_device_ids=true, to_apply=%add | all-reduce | flops 128 | bytes 1024
  158.6 4.4 broadcast.106.clone.1
  163.0 20.7 %while.69 = (s32[]{:T(128)}, f32[16]{0:T(128)S(1)}, f32[16,128,128]{2,1,0:T(8,128)S(1)}, f32[8,16]{1,0:T(8,128)S(1)}, f32[8,16,128,128]{3,2,1,0:T(8,128)}, /*ind...) while((s32[]{:T(128)}, f32[16]{0:T(128)S(1)}, ...), condition=%wide.region_9.10_spmd.clone, body=%wide.region_8.9_spmd.clone.sunk | while | flops 1048612 | bytes 5243533 | solution.py:189
  184.8 4.3 broadcast.106.clone
  189.1 20.8 %while.68 = (s32[]{:T(128)}, f32[16]{0:T(128)S(1)}, f32[16,128,128]{2,1,0:T(8,128)S(1)}, f32[8,16]{1,0:T(8,128)S(1)}, f32[8,16,128,128]{3,2,1,0:T(8,128)}, /*ind...) while((s32[]{:T(128)}, f32[16]{0:T(128)S(1)}, ...), condition=%wide.region_2.3_spmd.clone, body=%wide.region_1.2_spmd.clone.sunk | while | flops 1048611 | bytes 5244021 | solution.py:188
  215.6 3.0 collective-permute-start
  225.6 2.9 fusion.70
  228.5 3.3 convolution_bitcast_fusion
  234.0 4.7 collective-permute-start.3
  238.7 2.5 fusion.44
  241.2 4.8 convolution_bitcast_fusion.1
  251.1 75.5 %all-reduce.3 = (f32[512]{0:T(512)S(1)}, f32[512]{0:T(512)S(1)}) all-reduce(f32[512]{0:T(512)S(1)} %dynamic-update-slice.7, f32[512]{0:T(512)S(1)} %dynamic-update-slice.8), channel_id=4, replica_groups=mesh['outer'=32,'inner'=8] {'outer'}, use_global_device_ids=true, to_apply=%add.1 | all-reduce | flops 1024 | bytes 8192
  326.8 95.9 %all-gather.14.cloned.1.call-done = f32[512,128,128]{2,1,0:T(8,128)} async-done(((f32[16,128,128]{2,1,0:T(8,128)}), f32[512,128,128]{2,1,0:T(8,128)}) %all-gather.14.cloned.1.call-update) | async-done | bytes 33554448 | tf_op jit(solution)/shard_map/all_gather | solution.py:19
  423.0 3.3 convolution_bitcast_fusion.4
  430.2 7.0 scatter-add.9
  439.7 2.7 convolution_bitcast_fusion.5
  444.1 5.1 scatter-add.6
  450.4 203.7 %all-gather.12.cloned.1.call-done = f32[512,128,128]{2,1,0:T(8,128)} async-done(((f32[16,128,128]{2,1,0:T(8,128)}), f32[512,128,128]{2,1,0:T(8,128)}) %all-gather.12.cloned.1.call-update) | async-done | bytes 33554448 | tf_op jit(solution)/shard_map/all_gather | solution.py:19
  654.1 46.8 %while.66 = (s32[]{:T(128)}, f32[16,128,128]{2,1,0:T(8,128)S(1)}, s32[]{:T(128)}, f32[32,16]{1,0:T(8,128)S(1)}, f32[32,16,128,128]{3,2,1,0:T(8,128)}, /*index=5*/s32[]{:T(128)}, s32[]{:T(128)}, s32[]{:T(128)}) while((s32[]{:T(128)}, f32[16,128,128]{2,1,0:T(8,128)S(1)}, s32[]{:T(128)}, f32[32,16]{1,0:T(8,128)S(1)}, ...), condition=%wide.region_4.5_spmd, body=%wide.region_3.4_spmd.sunk | while | flops 524293 | bytes 3146047 | solution.py:28
  700.9 3.6 fusion.20
  704.5 4.3 fusion.26
  710.2 4.2 fusion.22
  (232 shorter events, 131.0 us)
Async XLA Ops:
  7.2 177.6 %all-gather.10.cloned.1.call-start = ((), (), s32[]{:S(2)}) async-start(), calls=%async_computation.1 | async-start | bytes 9437184 | tf_op jit(solution)/shard_map/all_gather | solution.py:181
  11.1 2.3 copy-start.13
  13.4 1.0 copy-start.14
  20.2 5.3 copy-start.17
  20.2 138.4 %all-to-all-start = ((f32[8,1,16,128,128]{4,3,2,1,0:T(8,128)}), f32[8,1,16,128,128]{4,3,2,1,0:T(8,128)}, u32[]{:S(2)}, u32[]{:S(2)}) async-start(f32[8,1,16,128,128]{4,3,2,1,0:T(8,128)} %stack.3), calls=%async_computation | async-start | bytes 16777216 | tf_op jit(solution)/shard_map/all_to_all | solution.py:183
  25.4 397.3 %all-gather.14.cloned.1.call-start = ((), (), s32[]{:S(2)}) async-start(), calls=%async_computation.3 | async-start | bytes 34603008 | tf_op jit(solution)/shard_map/all_gather | solution.py:19
  184.7 469.3 %all-gather.12.cloned.1.call-start = ((), (), s32[]{:S(2)}) async-start(), calls=%async_computation.2 | async-start | bytes 34603008 | tf_op jit(solution)/shard_map/all_gather | solution.py:19
  211.0 9.0 %copy-start.16 = (u32[256]{0:T(256)S(1)}, u32[256]{0:T(256)}, u32[]{:S(2)}) copy-start(u32[256]{0:T(256)} %constant.203) | copy-start | bytes 3076
  212.7 12.9 %collective-permute-start.1 = (bf16[64,16,128]{2,0,1:T(8,128)(2,1)}, bf16[64,16,128]{2,0,1:T(8,128)(2,1)}, u32[]{:S(2)}, u32[]{:S(2)}) collective-permute-start(bf16[64,16,128]{2,0,1:T(8,128)(2,1)} %copy_bitcast_fusion), channel_id=1, source_target_pairs={{0,1},{1,2},{2,3},{3,4},{4,5},{5,6},{6,7},{7,8},{8,9},{9,10},{10,1... | collective-permute-start | bytes 786440 | tf_op jit(solution)/shard_map/ppermute | solution.py:12
  215.6 23.1 %collective-permute-start = (bf16[64,16,128]{2,0,1:T(8,128)(2,1)S(1)}, bf16[64,16,128]{2,0,1:T(8,128)(2,1)}, u32[]{:S(2)}, u32[]{:S(2)}) collective-permute-start(bf16[64,16,128]{2,0,1:T(8,128)(2,1)S(1)} %copy_bitcast_fusion.1), channel_id=1, source_target_pairs={{0,1},{1,2},{2,3},{3,4},{4,5},{5,6},{6,7},{7,8},{8,9},{9,10},{10,1... | collective-permute-start | bytes 786440 | tf_op jit(solution)/shard_map/ppermute | solution.py:12
  219.9 18.8 %copy-start.5 = (bf16[128,16,128]{2,0,1:T(8,128)(2,1)}, bf16[128,16,128]{2,0,1:T(8,128)(2,1)S(1)}, u32[]{:S(2)}) copy-start(bf16[128,16,128]{2,0,1:T(8,128)(2,1)S(1)} %copy.82) | copy-start | bytes 1572868
  222.0 2.1 copy-start.9
  222.5 3.1 copy-start.7
  225.6 2.9 copy-start.15
  234.0 192.8 %collective-permute-start.3 = (bf16[64,16,128]{0,2,1:T(8,128)(2,1)}, bf16[64,16,128]{0,2,1:T(8,128)(2,1)}, u32[]{:S(2)}, u32[]{:S(2)}) collective-permute-start(bf16[64,16,128]{0,2,1:T(8,128)(2,1)} %slice.107), channel_id=1, source_target_pairs={{1,0},{2,1},{3,2},{4,3},{5,4},{6,5},{7,6},{8,7},{9,8},{10,9},{11,1... | collective-permute-start | bytes 786440 | tf_op jit(solution)/shard_map/ppermute | solution.py:12
  248.1 194.6 %collective-permute-start.2 = (bf16[64,16,128]{0,2,1:T(8,128)(2,1)}, bf16[64,16,128]{0,2,1:T(8,128)(2,1)}, u32[]{:S(2)}, u32[]{:S(2)}) collective-permute-start(bf16[64,16,128]{0,2,1:T(8,128)(2,1)} %slice.108), channel_id=1, source_target_pairs={{1,0},{2,1},{3,2},{4,3},{5,4},{6,5},{7,6},{8,7},{9,8},{10,9},{11,1... | collective-permute-start | bytes 786440 | tf_op jit(solution)/shard_map/ppermute | solution.py:12
  423.0 3.4 copy-start.10
  423.0 3.4 copy-start.12
  426.8 1.0 copy-start.2
  439.7 2.7 copy-start.8
  439.7 2.7 copy-start.11
  654.1 46.8 %copy-start.4 = (f32[128,16,128]{0,2,1:T(8,128)S(1)}, f32[128,16,128]{0,2,1:T(8,128)}, u32[]{:S(2)}) copy-start(f32[128,16,128]{0,2,1:T(8,128)} %convolution_bitcast_fusion.7) | copy-start | bytes 3145732
  708.8 1.4 copy-start.3
  710.2 4.2 copy-start.6
  (2 other events, 2.0 us)
Sparse Core Ops, SparseCore 0:
  13.5 96.9 all-gather.9
  184.8 237.7 all-gather.13
  425.3 228.7 all-gather.11
